TPU v7x, 32 devices: a whole 2x2x4 slice. The times are simulated.
32 devices in a mesh: groups: 2 (over y), seq: 4 (over z), inner: 2 (over x), head: 2 (over core).
Axes of the slice: x: 2, y: 2, z: 4, core: 2. Of those that a mesh axis runs over, the one named last changes fastest.
Arguments:
- queries: bfloat16 [2048, 32, 128], P(('groups', 'seq', 'inner'), 'head'), parts along dimension 0, as said below
- keys: bfloat16 [2048, 4, 128], P(('groups', 'seq', 'inner'), 'head'), parts along dimension 0
- values: bfloat16 [2048, 4, 128], P(('groups', 'seq', 'inner'), 'head'), parts along dimension 0, may hold values from -6 to 6
- log_decay: float32 [2048, 4], P(('groups', 'seq', 'inner'), 'head'), parts along dimension 0, as said below
- gain: float32 [32, 128], P('head'), may hold values from 0.1 to 1.9
- block_list: int32 [32, 16], P(('groups', 'seq', 'inner')), parts along dimension 0, may hold values from 0 to 15, as said below
Outputs:
- attended: bfloat16 [2048, 32, 128], P(('groups', 'seq', 'inner'), 'head'), parts along dimension 0
There are 2 independent parts, one for each index of `groups`. A program takes and returns all parts, laid end to end along the dimension named above; an argument that names none is the same for every part. Nothing has to cross between parts.
Inputs may be any that keep to these rules, and one draw needn't show every extreme that they name: Keys lie within -6 to 6; queries within -144 to 144. `log_decay`: each entry is below 0. `block_list`: entry 0 of row b is b. The sequence's pieces of 128 tokens fall into segments: piece p belongs to segment p modulo 2. Every entry of row b is a block at or before b in a piece of b's segment.
All inputs are finite; a program needn't handle non-finite values.
Results may differ from a plain program's by a relative error of at most 0.0017.
Values may be sent and summed in bfloat16 or wider, within the bound.
A program may use at most 64 MiB of HBM per device.

v0:
```python
import jax
import jax.numpy as jnp
from jax import lax
from jax.sharding import PartitionSpec as P

BLK = 64
SEL = 16
HIGH = lax.Precision.HIGHEST


def prefix(shard, axis, combine, identity):
    devices, here = (lax.axis_size(axis), lax.axis_index(axis))
    everything = jax.tree.map(lambda part: lax.all_gather(part, axis), shard)
    start = jax.tree.map(
        lambda part, zero: jnp.broadcast_to(jnp.asarray(zero, part.dtype), part.shape),
        shard,
        identity,
    )

    def turn(k, before):
        reached = k < here
        new = combine(before, jax.tree.map(lambda part: part[k], everything))
        return jax.tree.map(lambda a, b: jnp.where(reached, a, b), new, before)

    return lax.fori_loop(0, devices, turn, start)


def combine(earlier, later):
    return (earlier[0] * later[0], later[0][:, None, None] * earlier[1] + later[1])


def shards(queries, keys, values, log_decay, gain, block_list):
    tokens, heads_loc, width = queries.shape
    kv_loc = keys.shape[1]
    rep = heads_loc // kv_loc
    qf = queries.astype(jnp.float32).reshape(tokens, kv_loc, rep, width)
    kf = keys.astype(jnp.float32)
    vf = values.astype(jnp.float32)
    cum = jnp.cumsum(log_decay, axis=0)
    total = cum[-1]
    causal = jnp.arange(tokens)[:, None] >= jnp.arange(tokens)[None, :]
    scores = jnp.einsum("tkrd,skd->krts", qf, kf, precision=HIGH)
    diff = cum.T[:, :, None] - cum.T[:, None, :]
    weight = jnp.where(causal[None], jnp.exp(jnp.minimum(diff, 0.0)), 0.0)
    intra = jnp.einsum("krts,skd->tkrd", scores * weight[:, None], vf, precision=HIGH)
    tail = jnp.exp(total[None, :] - cum)
    own_state = jnp.einsum("skd,ske->kde", kf * tail[:, :, None], vf, precision=HIGH)
    own_decay = jnp.exp(total)
    identity = (jnp.ones_like(own_decay), jnp.zeros_like(own_state))
    prior = prefix((own_decay, own_state), ("seq", "inner"), combine, identity)
    prior_state = prior[1]
    inter = jnp.exp(cum)[:, :, None, None] * jnp.einsum(
        "tkrd,kde->tkre", qf, prior_state, precision=HIGH
    )
    linear = (intra + inter).reshape(tokens, heads_loc, width)
    normed = (
        linear * lax.rsqrt(jnp.mean(linear * linear, axis=-1, keepdims=True) + 1e-06) * gain[None]
    )
    per_piece = tokens // BLK
    n_inner = lax.axis_size("inner")
    start_pos = (lax.axis_index("seq") * n_inner + lax.axis_index("inner")) * tokens
    seg_block = block_list // (n_inner * per_piece) * per_piece + block_list % per_piece
    seg_keys, seg_values = (
        lax.all_gather(keys, "seq", axis=0, tiled=True),
        lax.all_gather(values, "seq", axis=0, tiled=True),
    )
    key_blocks = seg_keys.reshape(-1, BLK, kv_loc, width)
    value_blocks = seg_values.reshape(-1, BLK, kv_loc, width)
    picked_keys = key_blocks[seg_block]
    picked_values = value_blocks[seg_block]
    lower = jnp.arange(SEL)[None, :] < jnp.arange(SEL)[:, None]
    repeat = jnp.any((block_list[:, :, None] == block_list[:, None, :]) & lower[None], axis=2)
    keep_all = jnp.logical_not(repeat)
    query_pos = start_pos + jnp.arange(tokens).reshape(per_piece, BLK)
    key_pos = block_list[:, :, None] * BLK + jnp.arange(BLK)[None, None, :]
    q_blocks = queries.reshape(per_piece, BLK, kv_loc, rep, width)

    def one_block(args):
        qblk, pk, pv, qpos, kpos, keep = args
        valid = keep[None, :, None] & (kpos[None] <= qpos[:, None, None])
        score = jnp.einsum(
            "qkrd,jukd->krqju", qblk, pk, preferred_element_type=jnp.float32
        ) * width ** (-0.5)
        score = jnp.where(valid[None, None], score, -1e30)
        top = jnp.max(score, axis=(3, 4), keepdims=True)
        expo = jnp.where(valid[None, None], jnp.exp(score - top), 0.0)
        denom = jnp.sum(expo, axis=(3, 4))
        weights = expo.astype(jnp.bfloat16)
        out = jnp.einsum("krqju,jukd->qkrd", weights, pv, preferred_element_type=jnp.float32)
        return out / jnp.transpose(denom, (2, 0, 1))[:, :, :, None]

    outs = lax.map(one_block, (q_blocks, picked_keys, picked_values, query_pos, key_pos, keep_all))
    sparse = outs.reshape(tokens, heads_loc, width)
    return (normed + sparse).astype(jnp.bfloat16)


def solution(mesh):
    return jax.shard_map(
        shards,
        mesh=mesh,
        in_specs=(
            P(("groups", "seq", "inner"), "head", None),
            P(("groups", "seq", "inner"), "head", None),
            P(("groups", "seq", "inner"), "head", None),
            P(("groups", "seq", "inner"), "head"),
            P("head", None),
            P(("groups", "seq", "inner"), None),
        ),
        out_specs=P(("groups", "seq", "inner"), "head", None),
        check_vma=False,
    )
```

profile of v0, /device:TPU:0, one launch (start us, length us, event | category | flops | bytes accessed | tf_op | source)
XLA Modules:
  0.0 109.6 jit_solution(16745564901405145584)
XLA Ops:
  6.5 0.8 copy.113
  7.3 0.2 reduce_window_sum.11
  7.5 0.6 slice_bitcast_fusion
  8.1 1.0 convert_multiply_fusion
  9.2 1.8 %fusion.30 = f32[2,128,128]{2,1,0:T(8,128)} fusion(f32[128,2,128]{2,1,0:T(2,128)S(1)} %convert_multiply_fusion, bf16[128,2,128]{2,1,0:T(2,128)(2,1)} %param.12), kind=kOutput, calls=%fused_computation.44 | convolution fusion | flops 50331648 | bytes 327680 | tf_op jit(solution)/shard_map/skd,ske->kde/dot_general | solution.py:47
  11.0 0.9 copy.121
  11.9 0.9 copy.129
  12.7 16.1 %all_gather.19 = bf16[512,2,128]{2,0,1:T(8,128)(2,1)S(1)} all-gather(bf16[128,2,128]{2,0,1:T(8,128)(2,1)S(1)} %copy.121), channel_id=1, replica_groups=mesh['groups'=2,'seq'=4,'inner'=2,'head'=2] {'seq'}, dimensions={0}, use_global_device_ids=true | all-gather | bytes 327680 | tf_op jit(solution)/shard_map/all_gather | solution.py:65
  28.8 0.7 broadcast_multiply_fusion
  29.6 0.9 and_reduce_fusion
  30.5 0.6 not.3
  31.2 0.6 add_add_fusion
  31.8 15.7 %all_gather.20 = bf16[512,2,128]{2,0,1:T(8,128)(2,1)S(1)} all-gather(bf16[128,2,128]{2,0,1:T(8,128)(2,1)S(1)} %copy.129), channel_id=1, replica_groups=mesh['groups'=2,'seq'=4,'inner'=2,'head'=2] {'seq'}, dimensions={0}, use_global_device_ids=true | all-gather | bytes 327680 | tf_op jit(solution)/shard_map/all_gather | solution.py:64
  47.5 0.7 gather_fusion
  48.2 0.9 gather_fusion.1
  49.2 18.8 %while.24 = (s32[]{:T(128)}, f32[2,64,2,8,128]{4,3,2,1,0:T(8,128)S(1)}, bf16[2,16,64,2,128]{4,2,3,1,0:T(8,128)(2,1)S(1)}, pred[2,16]{1,0:T(4,128)(4,1)}, s32[2,1...) while((s32[]{:T(128)}, ...), condition=%wide.region_8.9_spmd, body=%wide.region_5.8_spmd.sunk | while | flops 550762496 | bytes 18383788 | solution.py:92
  49.2 0.7 fusion.47
  49.9 0.7 fusion.48
  50.6 0.2 compare_and_fusion.2
  50.8 1.0 constant_dynamic-slice_fusion.7
  51.8 1.8 %fusion.49 = (f32[2,8,64]{2,1,0:T(8,128)S(1)}, f32[2,16,64,64,8]{3,2,4,1,0:T(8,128)S(1)}) fusion(pred[64,16,64]{0,2,1:T(8,128)(4,1)S(1)} %compare_and_fusion.2, bf16[1,64,2,8,128]{4,3,2,1,0:T(8,128)(2,1)S(1)} %constant_dynamic-slice_fusion.7, bf16[1,16,64,2,128]{4,2,3,1,0:T(8,128)(2,1)S(1)} %get-tuple-element.348), kind=kOutput, calls=%fused_computation.4.clone.1 | convolution fusion | flops 271580160 | bytes 5050368 | tf_op jit(solution)/shard_map/while/body/eval_jaxpr/qkrd,jukd->krqju/dot_general | solution.py:81
  53.6 2.3 %fusion.50 = f32[2,8,64]{2,1,0:T(8,128)S(1)} fusion(f32[2,16,64,64,8]{3,2,4,1,0:T(8,128)S(1)} %get-tuple-element.349, f32[2,8,64]{2,1,0:T(8,128)S(1)} %get-tuple-element.350, pred[64,16,64]{0,2,1:T(8,128)(4,1)S(1)} %compare_and_fusion.2), kind=kLoop, calls=%fused_computation.5.clone.1 | loop fusion | flops 5241856 | bytes 4268032 | tf_op jit(solution)/shard_map/while/body/eval_jaxpr/reduce_sum | solution.py:87
  55.9 2.3 %fusion.51 = f32[1,64,2,8,128]{4,1,3,2,0:T(8,128)S(1)} fusion(f32[2,16,64,64,8]{3,2,4,1,0:T(8,128)S(1)} %get-tuple-element.349, f32[2,8,64]{2,1,0:T(8,128)S(1)} %get-tuple-element.350, pred[64,16,64]{0,2,1:T(8,128)(4,1)S(1)} %compare_and_fusion.2, bf16[1,16,64,2,128]{4,2,3,1,0:T(8,128)(2,1)S(1)} %get-tuple-element.351, f32[64,2,8]{0,2,1:T(8,128)S(1)} %bitcast.148), kind=kOutput, calls=%fused_computation.11.clone.1 | convolution fusion | flops 273809408 | bytes 5316608 | tf_op jit(solution)/shard_map/while/body/eval_jaxpr/krqju,jukd->qkrd/dot_general | solution.py:89
  58.2 0.4 copy_dynamic-update-slice_fusion.2
  58.6 0.7 fusion.47
  59.3 0.7 fusion.48
  59.9 0.2 compare_and_fusion.2
  60.2 1.0 constant_dynamic-slice_fusion.7
  61.2 1.8 %fusion.49 = (f32[2,8,64]{2,1,0:T(8,128)S(1)}, f32[2,16,64,64,8]{3,2,4,1,0:T(8,128)S(1)}) fusion(pred[64,16,64]{0,2,1:T(8,128)(4,1)S(1)} %compare_and_fusion.2, bf16[1,64,2,8,128]{4,3,2,1,0:T(8,128)(2,1)S(1)} %constant_dynamic-slice_fusion.7, bf16[1,16,64,2,128]{4,2,3,1,0:T(8,128)(2,1)S(1)} %get-tuple-element.348), kind=kOutput, calls=%fused_computation.4.clone.1 | convolution fusion | flops 271580160 | bytes 5050368 | tf_op jit(solution)/shard_map/while/body/eval_jaxpr/qkrd,jukd->krqju/dot_general | solution.py:81
  63.0 2.3 %fusion.50 = f32[2,8,64]{2,1,0:T(8,128)S(1)} fusion(f32[2,16,64,64,8]{3,2,4,1,0:T(8,128)S(1)} %get-tuple-element.349, f32[2,8,64]{2,1,0:T(8,128)S(1)} %get-tuple-element.350, pred[64,16,64]{0,2,1:T(8,128)(4,1)S(1)} %compare_and_fusion.2), kind=kLoop, calls=%fused_computation.5.clone.1 | loop fusion | flops 5241856 | bytes 4268032 | tf_op jit(solution)/shard_map/while/body/eval_jaxpr/reduce_sum | solution.py:87
  65.3 2.3 %fusion.51 = f32[1,64,2,8,128]{4,1,3,2,0:T(8,128)S(1)} fusion(f32[2,16,64,64,8]{3,2,4,1,0:T(8,128)S(1)} %get-tuple-element.349, f32[2,8,64]{2,1,0:T(8,128)S(1)} %get-tuple-element.350, pred[64,16,64]{0,2,1:T(8,128)(4,1)S(1)} %compare_and_fusion.2, bf16[1,16,64,2,128]{4,2,3,1,0:T(8,128)(2,1)S(1)} %get-tuple-element.351, f32[64,2,8]{0,2,1:T(8,128)S(1)} %bitcast.148), kind=kOutput, calls=%fused_computation.11.clone.1 | convolution fusion | flops 273809408 | bytes 5316608 | tf_op jit(solution)/shard_map/while/body/eval_jaxpr/krqju,jukd->qkrd/dot_general | solution.py:89
  67.6 0.4 copy_dynamic-update-slice_fusion.2
  68.0 20.6 %all-gather.1 = f32[8,1,2]{2,1,0:T(1,128)S(1)} all-gather(f32[1,1,2]{2,1,0:T(1,128)S(1)} %copy-done.4), channel_id=1, replica_groups=mesh['groups'=2,'seq'=4,'inner'=2,'head'=2] {'seq','inner'}, dimensions={0}, use_global_device_ids=true | all-gather | bytes 72 | tf_op jit(solution)/shard_map/all_gather | solution.py:13
  88.7 0.1 exponential_select_fusion.1
  88.9 1.4 %fusion.26 = f32[2,8,128,128]{2,3,1,0:T(8,128)S(1)} fusion(f32[2,128,128]{1,2,0:T(8,128)S(1)} %exponential_select_fusion.1, bf16[128,2,8,128]{3,2,1,0:T(8,128)(2,1)} %bitcast.138, bf16[128,2,128,1]{2,1,0,3:T(2,128)(2,1)S(1)} %bitcast.144), kind=kOutput, calls=%fused_computation.38 | convolution fusion | flops 67371008 | bytes 1769472 | tf_op jit(solution)/shard_map/tkrd,skd->krts/dot_general | solution.py:42
  90.2 0.7 convolution_bitcast_fusion.2
  91.0 8.3 %while.25 = (s32[]{:T(128)}, f32[2,128,128]{2,1,0:T(8,128)S(1)}, s32[]{:T(128)}, f32[8,2]{1,0:T(8,128)S(1)}, f32[8,2,128,128]{3,2,1,0:T(8,128)}, /*index=5*/s32[]{:T(128)}, s32[]{:T(128)}) while((s32[]{:T(128)}, f32[2,128,128]{2,1,0:T(8,128)S(1)}, s32[]{:T(128)}, f32[8,2]{1,0:T(8,128)S(1)}, f32[8,2,128,128]{3,2,1,0:T(8,128)}, ...), condition=%wide.region_2.3_spmd.clone, body=%wide.region_1.2_spmd.clone.sunk | while | flops 131076 | bytes 393353 | solution.py:25
  91.0 1.0 fusion.52
  92.0 1.0 fusion.52
  93.1 1.0 fusion.52
  94.1 1.0 fusion.52
  95.1 1.0 fusion.52
  96.2 1.0 fusion.52
  97.2 1.0 fusion.52
  98.2 1.0 fusion.52
  99.2 1.8 %multiply_reduce_fusion = (f32[128,2,8]{0,2,1:T(8,128)S(1)}, f32[128,2,8,128]{0,3,2,1:T(8,128)S(1)}) fusion(f32[128,2,8,128]{0,3,2,1:T(8,128)S(1)} %convolution_bitcast_fusion.2, bf16[128,2,8,128]{3,2,1,0:T(8,128)(2,1)} %bitcast.139, f32[2,128,128]{2,1,0:T(8,128)S(1)} %get-tuple-element.141, f32[128,2]{0,1:T(2,128)S(1)} %copy.118), kind=kOutput, calls=%fused_computation.40 | convolution fusion | flops 403699712 | bytes 2761728 | tf_op jit(solution)/shard_map/tkrd,kde->tkre/dot_general | solution.py:52
  101.0 0.5 copy.126
  101.6 1.1 %add_convert_fusion = bf16[128,16,128]{2,1,0:T(8,128)(2,1)} fusion(f32[128,16,128]{2,1,0:T(8,128)S(1)} %bitcast.143, f32[128,16,128]{2,1,0:T(8,128)S(1)} %copy.126, f32[16,128]{1,0:T(8,128)S(1)} %copy-done.3, f32[128,16]{1,0:T(8,128)S(1)} %copy.125), kind=kLoop, calls=%fused_computation.39 | loop fusion | flops 1048576 | bytes 2637824 | tf_op jit(solution)/shard_map/convert_element_type | solution.py:94
  (39 shorter events, 0.8 us)
Async XLA Ops:
  6.5 84.4 %all-gather.4.cloned.1.call-start = ((), (), s32[]{:S(2)}) async-start(), calls=%async_computation | async-start | bytes 1179648 | tf_op jit(solution)/shard_map/all_gather | solution.py:13
  29.6 17.9 %copy-start.2 = (s32[1024]{0:T(1024)}, s32[1024]{0:T(1024)S(1)}, u32[]{:S(2)}) copy-start(s32[1024]{0:T(1024)S(1)} %pad_clamp_fusion) | copy-start | bytes 12292
  49.1 18.8 %copy-start.4 = (f32[1,1,2]{2,1,0:T(1,128)S(1)}, f32[1,1,2]{2,1,0:T(1,128)}, u32[]{:S(2)}) copy-start(f32[1,1,2]{2,1,0:T(1,128)} %get-tuple-element.264) | copy-start | bytes 28
  49.1 39.7 %copy-start = (bf16[128,2,128]{2,1,0:T(2,128)(2,1)S(1)}, bf16[128,2,128]{2,1,0:T(2,128)(2,1)}, u32[]{:S(2)}) copy-start(bf16[128,2,128]{2,1,0:T(2,128)(2,1)} %param.11) | copy-start | bytes 196612
  49.2 41.1 %copy-start.1 = (bf16[128,2,128]{2,1,0:T(2,128)(2,1)S(1)}, bf16[128,2,128]{2,1,0:T(2,128)(2,1)}, u32[]{:S(2)}) copy-start(bf16[128,2,128]{2,1,0:T(2,128)(2,1)} %param.12) | copy-start | bytes 196612
  67.9 33.7 %copy-start.3 = (f32[16,128]{1,0:T(8,128)S(1)}, f32[16,128]{1,0:T(8,128)}, u32[]{:S(2)}) copy-start(f32[16,128]{1,0:T(8,128)} %param.14) | copy-start | bytes 24580
Sparse Core Ops, SparseCore 0:
  11.1 43.3 all-gather.3
where the time goes:
time: 110 us
  blocking collectives  52.4 us (48%)
  other arithmetic  18.3 us (17%)
  matrix products  13.7 us (12%)
  between operations  13.6 us (12%)
  local copies, waits for them, and re-layouts  11.2 us (10%)
    all_gather x1, blocking collectives, prefix(): everything = jax.tree.map(lambda part: lax.all_gather(part, axis), shard)  20.6 us
    all_gather x1, blocking collectives, shards(): lax.all_gather(values, 'seq', axis=0, tiled=True)  16.1 us
    all_gather x1, blocking collectives, shards(): lax.all_gather(keys, 'seq', axis=0, tiled=True)  15.7 us
    select_n x8, other arithmetic, turn(): return jax.tree.map(lambda a, b: jnp.where(reached, a, b), new, before)  7.94 us
    dot_general x2, matrix products, one_block(): jnp.einsum('krqju,jukd->qkrd', weights, pv, preferred_element_type=jnp.fl...  4.6 us
    reduce_sum x2, other arithmetic, one_block(): denom = jnp.sum(expo, axis=(3, 4))  4.54 us
    dot_general x2, matrix products, one_block(): jnp.einsum('qkrd,jukd->krqju', qblk, pk, preferred_element_type=jnp.float32)  3.54 us
    unnamed x13, local copies, waits for them, and re-layouts  2.52 us
  transfers between devices with their start and end apart: 1, of which 0 were waited for; matrix products, arithmetic and copies ran while one was open for 25% of the time, Pallas kernels for 0%

commit v1 on v0

--- a/solution.py
+++ b/solution.py
@@ -1,3 +1,4 @@
+import functools
 import jax
 import jax.numpy as jnp
 from jax import lax
@@ -6,6 +7,41 @@
 BLK = 64
 SEL = 16
 HIGH = lax.Precision.HIGHEST
+
+
+def supply_all_the_ports(tile_in, array_dim):
+    tile_in = jnp.moveaxis(tile_in, 0, array_dim)
+    wide_out = tile_in.shape
+    return tile_in.reshape(
+        *wide_out[:array_dim],
+        wide_out[array_dim] * wide_out[array_dim + 1],
+        *wide_out[array_dim + 2 :]
+    )
+
+
+def cover_turns_all(local_block, dim_at, shard_axis):
+    axis_len = lax.axis_size(shard_axis)
+    parts_seen = tuple(((no, (no + 1) % axis_len) for no in range(axis_len)))
+    all_rows = tuple(((rr, dd) for dd, rr in parts_seen))
+    outcome_arr, z2 = ([], [])
+    i = 0
+    while i < axis_len - 1:
+        if i % 2 == 0:
+            outcome_arr.append(
+                lax.ppermute(
+                    outcome_arr[-1] if outcome_arr else local_block, shard_axis, parts_seen
+                )
+            )
+        else:
+            z2.append(lax.ppermute(z2[-1] if z2 else local_block, shard_axis, all_rows))
+        i += 1
+    near = jnp.stack([*outcome_arr[::-1], local_block, *z2])
+    aux = lax.axis_index(shard_axis) - len(outcome_arr)
+    near = near[(jnp.arange(axis_len) - aux) % axis_len]
+    return supply_all_the_ports(near, dim_at)
+
+
+step_on_quotas_here = functools.partial(cover_turns_all, dim_at=0, shard_axis="seq")
 
 
 def prefix(shard, axis, combine, identity):
@@ -62,7 +98,7 @@
     seg_block = block_list // (n_inner * per_piece) * per_piece + block_list % per_piece
     seg_keys, seg_values = (
         lax.all_gather(keys, "seq", axis=0, tiled=True),
-        lax.all_gather(values, "seq", axis=0, tiled=True),
+        step_on_quotas_here(values),
     )
     key_blocks = seg_keys.reshape(-1, BLK, kv_loc, width)
     value_blocks = seg_values.reshape(-1, BLK, kv_loc, width)

time: 110 us -> 105 us (0.955)
  blocking collectives: 52.4 us -> 36.1 us
  waiting for transfers between devices: 0.04 us -> 6.05 us
  starting transfers between devices: 0.01 us -> 5.19 us
  local copies, waits for them, and re-layouts: 11.2 us -> 8.55 us
  matrix products: 13.7 us -> 15.8 us
    all_gather x1 -> x0, blocking collectives: 16.1 us -> none  [shards(): lax.all_gather(values, 'seq', axis=0, tiled=True)]
    ppermute x0 -> x3, waiting for transfers between devices: none -> 6.03 us  [the longest x2 6.03 us: cover_turns_all(): lax.ppermute(outcome_arr[-1] if outcome_arr else local_block, shard_axis,...]
    ppermute x0 -> x3, starting transfers between devices: none -> 5.19 us  [the longest x1 5.13 us: cover_turns_all(): z2.append(lax.ppermute(z2[-1] if z2 else local_block, shard_axis, all_rows))]
    while x0 -> x8, local copies, waits for them, and re-layouts: none -> 1.99 us
    dynamic_slice x4, local copies, waits for them, and re-layouts: 2.11 us -> 0.21 us  [shards(): lax.map(one_block, (q_blocks, picked_keys, picked_values, query_pos, key_...]
    dot_general x1, matrix products: 0.68 us -> 2.54 us  [shards(): jnp.einsum('krts,skd->tkrd', scores * weight[:, None], vf, precision=HIGH)]
    le x4, local copies, waits for them, and re-layouts: 1.38 us -> 0.02 us  [one_block(): valid = keep[None, :, None] & (kpos[None] <= qpos[:, None, None])]
    and x2, local copies, waits for them, and re-layouts: 1.34 us -> 0.02 us  [one_block(): valid = keep[None, :, None] & (kpos[None] <= qpos[:, None, None])]
  transfers between devices with their start and end apart: 1 -> 4, of which waited for: 0 -> 1; matrix products, arithmetic and copies ran while one was open for 25% -> 26% of each run, Pallas kernels for 0% -> 0%
where the time goes in v1:
time: 105 us; the launch traced here: 104 us
  blocking collectives  36.1 us (34%)
  other arithmetic  18.4 us (18%)
  matrix products  15.8 us (15%)
  between operations  13.6 us (13%)
  local copies, waits for them, and re-layouts  8.55 us (8%)
  waiting for transfers between devices  6.05 us (6%)
  starting transfers between devices  5.19 us (5%)
    all_gather x1, blocking collectives, prefix(): everything = jax.tree.map(lambda part: lax.all_gather(part, axis), shard)  21.2 us
    all_gather x1, blocking collectives, shards(): lax.all_gather(keys, 'seq', axis=0, tiled=True)  15 us
    select_n x8, other arithmetic, turn(): return jax.tree.map(lambda a, b: jnp.where(reached, a, b), new, before)  7.94 us
    ppermute x2, waiting for transfers between devices, cover_turns_all(): lax.ppermute(outcome_arr[-1] if outcome_arr else local_block, shard_axis,...  6.03 us
    ppermute x1, starting transfers between devices, cover_turns_all(): z2.append(lax.ppermute(z2[-1] if z2 else local_block, shard_axis, all_rows))  5.13 us
    dot_general x2, matrix products, one_block(): jnp.einsum('krqju,jukd->qkrd', weights, pv, preferred_element_type=jnp.fl...  4.55 us
    reduce_sum x2, other arithmetic, one_block(): denom = jnp.sum(expo, axis=(3, 4))  4.53 us
    dot_general x2, matrix products, one_block(): jnp.einsum('qkrd,jukd->krqju', qblk, pk, preferred_element_type=jnp.float32)  3.55 us
  transfers between devices with their start and end apart: 4, of which 1 were waited for; matrix products, arithmetic and copies ran while one was open for 26% of the time, Pallas kernels for 0%

profile of v1, /device:TPU:0, one launch (start us, length us, event | category | flops | bytes accessed | tf_op | source)
XLA Modules:
  0.0 104.1 jit_solution(13668913398350411721)
XLA Ops:
  6.5 0.9 copy.221
  7.4 5.1 %collective-permute-start.2 = (bf16[128,2,128]{2,0,1:T(8,128)(2,1)S(1)}, bf16[128,2,128]{2,0,1:T(8,128)(2,1)S(1)}, u32[]{:S(2)}, u32[]{:S(2)}) collective-permute-start(bf16[128,2,128]{2,0,1:T(8,128)(2,1)S(1)} %copy.221), channel_id=1, source_target_pairs={{4,0},{8,4},{12,8},{0,12},{5,1},{9,5},{13,9},{1,13},{6,2},{10,6},{... | collective-permute-start | bytes 196616 | tf_op jit(solution)/shard_map/ppermute | solution.py:36
  12.6 0.8 copy.143
  13.4 0.2 reduce_window_sum.11
  13.6 1.0 convert_multiply_fusion
  14.6 1.8 %fusion.30 = f32[2,128,128]{2,1,0:T(8,128)} fusion(f32[128,2,128]{2,1,0:T(2,128)S(1)} %convert_multiply_fusion, bf16[128,2,128]{2,1,0:T(2,128)(2,1)} %param.12), kind=kOutput, calls=%fused_computation.46 | convolution fusion | flops 50331648 | bytes 327680 | tf_op jit(solution)/shard_map/skd,ske->kde/dot_general | solution.py:83
  16.5 0.9 copy.162
  17.4 0.7 broadcast_multiply_fusion
  18.1 0.1 reshape.172
  18.2 0.9 and_reduce_fusion
  19.1 0.1 iota_add_fusion
  19.2 15.0 %all_gather.16 = bf16[512,2,128]{2,0,1:T(8,128)(2,1)S(1)} all-gather(bf16[128,2,128]{2,0,1:T(8,128)(2,1)S(1)} %copy.162), channel_id=1, replica_groups=mesh['groups'=2,'seq'=4,'inner'=2,'head'=2] {'seq'}, dimensions={0}, use_global_device_ids=true | all-gather | bytes 327680 | tf_op jit(solution)/shard_map/all_gather | solution.py:100
  34.2 21.2 %all-gather.1 = f32[8,1,2]{2,1,0:T(1,128)S(1)} all-gather(f32[1,1,2]{2,1,0:T(1,128)S(1)} %get-tuple-element.277), channel_id=1, replica_groups=mesh['groups'=2,'seq'=4,'inner'=2,'head'=2] {'seq','inner'}, dimensions={0}, use_global_device_ids=true | all-gather | bytes 72 | tf_op jit(solution)/shard_map/all_gather | solution.py:49
  55.5 0.8 gather_fusion.2
  56.2 0.1 exponential_select_fusion.1
  56.4 1.4 %fusion.26 = f32[2,8,128,128]{2,3,1,0:T(8,128)S(1)} fusion(f32[2,128,128]{1,2,0:T(8,128)S(1)} %exponential_select_fusion.1, bf16[128,2,8,128]{3,2,1,0:T(8,128)(2,1)} %bitcast.145, bf16[128,2,128,1]{2,1,0,3:T(2,128)(2,1)} %bitcast.152), kind=kOutput, calls=%fused_computation.39 | convolution fusion | flops 67371008 | bytes 1769472 | tf_op jit(solution)/shard_map/tkrd,skd->krts/dot_general | solution.py:78
  57.8 2.5 %convolution_bitcast_fusion.2 = f32[128,2,8,128]{0,3,2,1:T(8,128)} fusion(f32[2,8,128,128]{2,3,1,0:T(8,128)S(1)} %fusion.26, bf16[128,2,128,1]{2,1,0,3:T(2,128)(2,1)} %bitcast.153), kind=kOutput, calls=%fused_computation.38 | convolution fusion | flops 402653184 | bytes 2162688 | tf_op jit(solution)/shard_map/krts,skd->tkrd/dot_general | solution.py:81
  60.4 6.0 %collective-permute-done.1 = bf16[128,2,128]{2,0,1:T(8,128)(2,1)S(1)} collective-permute-done((bf16[128,2,128]{2,0,1:T(8,128)(2,1)S(1)}, bf16[128,2,128]{2,0,1:T(8,128)(2,1)S(1)}, u32[]{:S(2)}, u32[]{:S(2)}) %collective-permute-start.1) | collective-permute-done | bytes 65568 | tf_op jit(solution)/shard_map/ppermute | solution.py:31
  66.5 0.6 gather_fusion
  67.1 0.7 gather_fusion.1
  67.9 16.2 %while.24 = (s32[]{:T(128)}, f32[2,64,2,8,128]{4,3,2,1,0:T(8,128)}, bf16[2,16,64,2,128]{4,2,3,1,0:T(8,128)(2,1)S(1)}, pred[2,16]{1,0:T(4,128)(4,1)S(1)}, s32[2,1...) while((s32[]{:T(128)}, f32[2,64,2,8,128]{4,3,2,1,0:T(8,128)}, ...), condition=%wide.region_8.9_spmd, body=%wide.region_5.8_spmd.sunk | while | flops 550762496 | bytes 26772452 | solution.py:128
  68.0 0.2 compare_and_fusion.2
  68.2 0.1 constant_dynamic-slice_fusion.8
  68.3 1.8 %fusion.51 = (f32[2,8,64]{2,1,0:T(8,128)S(1)}, f32[2,16,64,64,8]{3,2,4,1,0:T(8,128)S(1)}) fusion(pred[64,16,64]{0,2,1:T(8,128)(4,1)S(1)} %compare_and_fusion.2, bf16[1,64,2,8,128]{4,3,2,1,0:T(8,128)(2,1)S(1)} %constant_dynamic-slice_fusion.7, bf16[1,16,64,2,128]{4,2,3,1,0:T(8,128)(2,1)S(1)} %get-tuple-element.363), kind=kOutput, calls=%fused_computation.5.clone.1 | convolution fusion | flops 271580160 | bytes 5050368 | tf_op jit(solution)/shard_map/while/body/eval_jaxpr/qkrd,jukd->krqju/dot_general | solution.py:117
  70.1 2.3 %fusion.52 = f32[2,8,64]{2,1,0:T(8,128)S(1)} fusion(f32[2,16,64,64,8]{3,2,4,1,0:T(8,128)S(1)} %get-tuple-element.364, f32[2,8,64]{2,1,0:T(8,128)S(1)} %get-tuple-element.365, pred[64,16,64]{0,2,1:T(8,128)(4,1)S(1)} %compare_and_fusion.2), kind=kLoop, calls=%fused_computation.6.clone.1 | loop fusion | flops 5241856 | bytes 4268032 | tf_op jit(solution)/shard_map/while/body/eval_jaxpr/reduce_sum | solution.py:123
  72.4 2.3 %fusion.53 = f32[1,64,2,8,128]{4,1,3,2,0:T(8,128)S(1)} fusion(f32[2,16,64,64,8]{3,2,4,1,0:T(8,128)S(1)} %get-tuple-element.364, f32[2,8,64]{2,1,0:T(8,128)S(1)} %get-tuple-element.365, pred[64,16,64]{0,2,1:T(8,128)(4,1)S(1)} %compare_and_fusion.2, bf16[1,16,64,2,128]{4,2,3,1,0:T(8,128)(2,1)S(1)} %get-tuple-element.366, f32[64,2,8]{0,2,1:T(8,128)S(1)} %bitcast.157), kind=kOutput, calls=%fused_computation.12.clone.1 | convolution fusion | flops 273809408 | bytes 5316608 | tf_op jit(solution)/shard_map/while/body/eval_jaxpr/krqju,jukd->qkrd/dot_general | solution.py:125
  74.7 0.4 copy_dynamic-update-slice_fusion.2
  75.0 1.0 copy-done.2
  76.0 0.2 compare_and_fusion.2
  76.3 0.1 constant_dynamic-slice_fusion.8
  76.4 1.8 %fusion.51 = (f32[2,8,64]{2,1,0:T(8,128)S(1)}, f32[2,16,64,64,8]{3,2,4,1,0:T(8,128)S(1)}) fusion(pred[64,16,64]{0,2,1:T(8,128)(4,1)S(1)} %compare_and_fusion.2, bf16[1,64,2,8,128]{4,3,2,1,0:T(8,128)(2,1)S(1)} %constant_dynamic-slice_fusion.7, bf16[1,16,64,2,128]{4,2,3,1,0:T(8,128)(2,1)S(1)} %get-tuple-element.363), kind=kOutput, calls=%fused_computation.5.clone.1 | convolution fusion | flops 271580160 | bytes 5050368 | tf_op jit(solution)/shard_map/while/body/eval_jaxpr/qkrd,jukd->krqju/dot_general | solution.py:117
  78.2 2.3 %fusion.52 = f32[2,8,64]{2,1,0:T(8,128)S(1)} fusion(f32[2,16,64,64,8]{3,2,4,1,0:T(8,128)S(1)} %get-tuple-element.364, f32[2,8,64]{2,1,0:T(8,128)S(1)} %get-tuple-element.365, pred[64,16,64]{0,2,1:T(8,128)(4,1)S(1)} %compare_and_fusion.2), kind=kLoop, calls=%fused_computation.6.clone.1 | loop fusion | flops 5241856 | bytes 4268032 | tf_op jit(solution)/shard_map/while/body/eval_jaxpr/reduce_sum | solution.py:123
  80.4 2.3 %fusion.53 = f32[1,64,2,8,128]{4,1,3,2,0:T(8,128)S(1)} fusion(f32[2,16,64,64,8]{3,2,4,1,0:T(8,128)S(1)} %get-tuple-element.364, f32[2,8,64]{2,1,0:T(8,128)S(1)} %get-tuple-element.365, pred[64,16,64]{0,2,1:T(8,128)(4,1)S(1)} %compare_and_fusion.2, bf16[1,16,64,2,128]{4,2,3,1,0:T(8,128)(2,1)S(1)} %get-tuple-element.366, f32[64,2,8]{0,2,1:T(8,128)S(1)} %bitcast.157), kind=kOutput, calls=%fused_computation.12.clone.1 | convolution fusion | flops 273809408 | bytes 5316608 | tf_op jit(solution)/shard_map/while/body/eval_jaxpr/krqju,jukd->qkrd/dot_general | solution.py:125
  82.7 0.4 copy_dynamic-update-slice_fusion.2
  83.1 1.0 copy-done.2
  84.1 8.3 %while.25 = (s32[]{:T(128)}, f32[2,128,128]{2,1,0:T(8,128)S(1)}, s32[]{:T(128)}, f32[8,2]{1,0:T(8,128)S(1)}, f32[8,2,128,128]{3,2,1,0:T(8,128)}, /*index=5*/s32[]{:T(128)}, s32[]{:T(128)}) while((s32[]{:T(128)}, f32[2,128,128]{2,1,0:T(8,128)S(1)}, s32[]{:T(128)}, f32[8,2]{1,0:T(8,128)S(1)}, f32[8,2,128,128]{3,2,1,0:T(8,128)}, ...), condition=%wide.region_2.3_spmd.clone, body=%wide.region_1.2_spmd.clone.sunk | while | flops 131076 | bytes 393353 | solution.py:61
  84.1 1.0 fusion.54
  85.1 1.0 fusion.54
  86.2 1.0 fusion.54
  87.2 1.0 fusion.54
  88.2 1.0 fusion.54
  89.3 1.0 fusion.54
  90.3 1.0 fusion.54
  91.4 1.0 fusion.54
  92.4 1.9 %multiply_reduce_fusion = (f32[128,2,8]{0,2,1:T(8,128)S(1)}, f32[128,2,8,128]{0,3,2,1:T(8,128)S(1)}) fusion(f32[128,2,8,128]{0,3,2,1:T(8,128)} %convolution_bitcast_fusion.2, bf16[128,2,8,128]{3,2,1,0:T(8,128)(2,1)S(1)} %bitcast.147, f32[2,128,128]{2,1,0:T(8,128)S(1)} %get-tuple-element.141, f32[128,2]{0,1:T(2,128)S(1)} %copy.148), kind=kOutput, calls=%fused_computation.41 | convolution fusion | flops 403699712 | bytes 2761728 | tf_op jit(solution)/shard_map/tkrd,kde->tkre/dot_general | solution.py:88
  94.3 0.5 copy.156
  94.8 0.1 copy.155
  94.9 2.4 %add_convert_fusion = bf16[128,16,128]{2,1,0:T(8,128)(2,1)} fusion(f32[128,16,128]{2,1,0:T(8,128)} %bitcast.151, f32[128,16,128]{2,1,0:T(8,128)S(1)} %copy.156, f32[16,128]{1,0:T(8,128)S(1)} %copy-done.3, f32[128,16]{1,0:T(8,128)S(1)} %copy.155), kind=kLoop, calls=%fused_computation.40 | loop fusion | flops 1048576 | bytes 2637824 | tf_op jit(solution)/shard_map/convert_element_type | solution.py:130
  (51 shorter events, 0.6 us)
Async XLA Ops:
  6.5 61.3 %copy-start = (bf16[128,16,128]{2,1,0:T(8,128)(2,1)S(1)}, bf16[128,16,128]{2,1,0:T(8,128)(2,1)}, u32[]{:S(2)}) copy-start(bf16[128,16,128]{2,1,0:T(8,128)(2,1)} %param.10) | copy-start | bytes 1572868
  6.5 77.6 %all-gather.4.cloned.1.call-start = ((), (), s32[]{:S(2)}) async-start(), calls=%async_computation | async-start | bytes 1179648 | tf_op jit(solution)/shard_map/all_gather | solution.py:49
  7.4 52.9 %collective-permute-start.2 = (bf16[128,2,128]{2,0,1:T(8,128)(2,1)S(1)}, bf16[128,2,128]{2,0,1:T(8,128)(2,1)S(1)}, u32[]{:S(2)}, u32[]{:S(2)}) collective-permute-start(bf16[128,2,128]{2,0,1:T(8,128)(2,1)S(1)} %copy.221), channel_id=1, source_target_pairs={{4,0},{8,4},{12,8},{0,12},{5,1},{9,5},{13,9},{1,13},{6,2},{10,6},{... | collective-permute-start | bytes 196616 | tf_op jit(solution)/shard_map/ppermute | solution.py:36
  12.6 47.7 %collective-permute-start = (bf16[128,2,128]{2,0,1:T(8,128)(2,1)S(1)}, bf16[128,2,128]{2,0,1:T(8,128)(2,1)S(1)}, u32[]{:S(2)}, u32[]{:S(2)}) collective-permute-start(bf16[128,2,128]{2,0,1:T(8,128)(2,1)S(1)} %copy.221), channel_id=1, source_target_pairs={{0,4},{4,8},{8,12},{12,0},{1,5},{5,9},{9,13},{13,1},{2,6},{6,10},{... | collective-permute-start | bytes 196616 | tf_op jit(solution)/shard_map/ppermute | solution.py:31
  60.3 6.1 %collective-permute-start.1 = (bf16[128,2,128]{2,0,1:T(8,128)(2,1)S(1)}, bf16[128,2,128]{2,0,1:T(8,128)(2,1)S(1)}, u32[]{:S(2)}, u32[]{:S(2)}) collective-permute-start(bf16[128,2,128]{2,0,1:T(8,128)(2,1)S(1)} %collective-permute-done), channel_id=1, source_target_pairs={{0,4},{4,8},{8,12},{12,0},{1,5},{5,9},{9,13},{13,1},{2,6},{6,10},{... | collective-permute-start | bytes 196616 | tf_op jit(solution)/shard_map/ppermute | solution.py:31
  67.9 27.1 %copy-start.3 = (f32[16,128]{1,0:T(8,128)S(1)}, f32[16,128]{1,0:T(8,128)}, u32[]{:S(2)}) copy-start(f32[16,128]{1,0:T(8,128)} %param.14) | copy-start | bytes 24580
  72.4 2.3 %copy-start.1 = (f32[2,64,2,8,128]{4,3,2,1,0:T(8,128)S(1)}, f32[2,64,2,8,128]{4,3,2,1,0:T(8,128)}, u32[]{:S(2)}) copy-start(f32[2,64,2,8,128]{4,3,2,1,0:T(8,128)} %get-tuple-element.382) | copy-start | bytes 3145732 | tf_op jit(solution)/shard_map/while
  75.0 1.0 copy-start.2
  80.4 2.3 %copy-start.1 = (f32[2,64,2,8,128]{4,3,2,1,0:T(8,128)S(1)}, f32[2,64,2,8,128]{4,3,2,1,0:T(8,128)}, u32[]{:S(2)}) copy-start(f32[2,64,2,8,128]{4,3,2,1,0:T(8,128)} %get-tuple-element.382) | copy-start | bytes 3145732 | tf_op jit(solution)/shard_map/while
  83.1 1.0 copy-start.2
Sparse Core Ops, SparseCore 0:
  16.6 42.4 all-gather.3
